TPU v7x, 32 devices: a whole 2x2x4 slice. The times are simulated.
32 devices in a mesh: groups: 2 (over x), wide: 16 (over z, y, core).
Axes of the slice: x: 2, y: 2, z: 4, core: 2. Of those that a mesh axis runs over, the one named last changes fastest.
Arguments:
- prefix_hidden: bfloat16 [32, 256, 8192], P(('groups', 'wide')), parts along dimension 0, may hold values from -6 to 6
- prefix_lengths: int32 [32], P(('groups', 'wide')), parts along dimension 0, may hold values from 64 to 256
- action_noise: float32 [32, 50, 32], P(('groups', 'wide')), parts along dimension 0, may hold values from -4 to 4
- prefix_gain: float32 [8192], replicated, may hold values from 0.1 to 1.9
- key_weight: bfloat16 [8192, 512], P('wide'), may hold values from -0.0625 to 0.0625
- value_weight: bfloat16 [8192, 512], P('wide'), may hold values from -0.0625 to 0.0625
- input_weight: float32 [32, 1024], replicated, may hold values from -1 to 1
- expert_gain: float32 [1024], replicated, may hold values from 0.1 to 1.9
- expert_query: bfloat16 [1024, 1024], P('wide'), may hold values from -0.1875 to 0.1875
- expert_key: bfloat16 [1024, 512], P('wide'), may hold values from -5.3125 to 5.3125
- expert_value: bfloat16 [1024, 512], P('wide'), may hold values from -0.1875 to 0.1875
- expert_output: bfloat16 [1024, 1024], P('wide'), may hold values from -0.1875 to 0.1875
- final_gain: float32 [1024], replicated, may hold values from 0.1 to 1.9
- output_weight: bfloat16 [1024, 32], replicated, may hold values from -0.1875 to 0.1875
Outputs:
- actions: float32 [32, 50, 32], P(('groups', 'wide')), parts along dimension 0
There are 2 independent parts, one for each index of `groups`. A program takes and returns all parts, laid end to end along the dimension named above; an argument that names none is the same for every part. Nothing has to cross between parts.
Inputs may be any that keep to these rules, and one draw needn't show every extreme that they name: `prefix_lengths`: positions at or after a sample's length are padding and take no part.
All inputs are finite; a program needn't handle non-finite values.
Results may differ from a plain program's by a relative error of at most 0.0075.
Values may be sent and summed in bfloat16 or wider, within the bound.
A program may use at most 128 MiB of HBM per device.

v0:
```python
import jax
import jax.numpy as jnp
from jax import lax
from jax.sharding import PartitionSpec as P

HEAD = 128
STEPS = 4
rope_base = 1000000.0
norm_eps = 1e-06


def normalize(values, norm_gain):
    mean_square = jnp.mean(values * values, axis=-1, keepdims=True)
    return values * lax.rsqrt(mean_square + norm_eps) * norm_gain


def rotate(values, positions):
    half_width = values.shape[-1] // 2
    inv_freqs = rope_base ** (-jnp.arange(half_width, dtype=jnp.float32) * 2.0 / values.shape[-1])
    angles = positions[:, None] * inv_freqs[None, :]
    cosine = jnp.cos(angles)[:, None, :]
    sine_part = jnp.sin(angles)[:, None, :]
    first_half = values[..., :half_width]
    second = values[..., half_width:]
    return jnp.concatenate(
        [first_half * cosine - second * sine_part, second * cosine + first_half * sine_part], -1
    )


def time_embedding(time_value, embed_width):
    half_width = embed_width // 2
    fraction = jnp.arange(half_width, dtype=jnp.float32) / (half_width - 1)
    period = 0.004 * (4.0 / 0.004) ** fraction
    angles = time_value * (2.0 * jnp.pi) / period
    return jnp.concatenate([jnp.sin(angles), jnp.cos(angles)])


def attend(queries, key_cache, value_cache, action_keys, action_values, is_valid):
    span_rows = queries.shape[0]
    groups = key_cache.shape[1] // HEAD
    group_ratio = queries.shape[1] // key_cache.shape[1]
    query_heads = queries.reshape(span_rows, groups, group_ratio, HEAD)
    prefix_keys = key_cache.reshape(-1, groups, HEAD)
    prefix_values = value_cache.reshape(-1, groups, HEAD)
    own_keys = action_keys.reshape(span_rows, groups, HEAD)
    own_values = action_values.reshape(span_rows, groups, HEAD)
    prefix_scores = jnp.einsum(
        "cgrh,pgh->grcp", query_heads, prefix_keys, preferred_element_type=jnp.float32
    )
    prefix_scores = jnp.where(is_valid[None, None, None, :], prefix_scores, -1e30)
    own_scores = jnp.einsum(
        "cgrh,ngh->grcn", query_heads, own_keys, preferred_element_type=jnp.float32
    )
    row_max = jnp.maximum(jnp.max(prefix_scores, -1), jnp.max(own_scores, -1))[..., None]
    prefix_exp = jnp.exp(prefix_scores - row_max)
    own_exp = jnp.exp(own_scores - row_max)
    prob_total = jnp.sum(prefix_exp, -1, keepdims=True) + jnp.sum(own_exp, -1, keepdims=True)
    prefix_prob = (prefix_exp / prob_total).astype(jnp.bfloat16)
    own_prob = (own_exp / prob_total).astype(jnp.bfloat16)
    attn_mixed = jnp.einsum(
        "grcp,pgh->cgrh", prefix_prob, prefix_values, preferred_element_type=jnp.float32
    )
    attn_mixed = attn_mixed + jnp.einsum(
        "grcn,ngh->cgrh", own_prob, own_values, preferred_element_type=jnp.float32
    )
    return attn_mixed.reshape(span_rows, -1).astype(jnp.bfloat16)


def expert_steps(
    noise_rows,
    length,
    input_weight,
    expert_gain,
    query_w,
    key_w,
    value_w,
    output_w,
    final_gain,
    output_weight,
    key_cache,
    value_cache,
):
    span_rows = noise_rows.shape[0]
    is_valid = jnp.arange(key_cache.shape[0], dtype=jnp.int32) < length
    positions = length.astype(jnp.float32) + jnp.arange(span_rows, dtype=jnp.float32)
    action_state = noise_rows
    for step_idx in range(STEPS):
        time_value = 1.0 - step_idx / STEPS
        hidden = jnp.dot(
            action_state,
            input_weight,
            precision=lax.Precision.HIGHEST,
            preferred_element_type=jnp.float32,
        )
        hidden = hidden + time_embedding(time_value, input_weight.shape[1])[None, :]
        normed = normalize(hidden, expert_gain).astype(jnp.bfloat16)
        raw_queries = jnp.dot(normed, query_w, preferred_element_type=jnp.float32)
        queries = rotate(raw_queries.reshape(span_rows, -1, HEAD), positions).reshape(span_rows, -1)
        queries = (queries * HEAD ** (-0.5)).astype(jnp.bfloat16)
        raw_keys = jnp.dot(normed, key_w, preferred_element_type=jnp.float32)
        action_keys = (
            rotate(raw_keys.reshape(span_rows, -1, HEAD), positions)
            .reshape(span_rows, -1)
            .astype(jnp.bfloat16)
        )
        action_values = jnp.dot(normed, value_w, preferred_element_type=jnp.float32).astype(
            jnp.bfloat16
        )
        attn_mixed = attend(queries, key_cache, value_cache, action_keys, action_values, is_valid)
        hidden = hidden + jnp.dot(attn_mixed, output_w, preferred_element_type=jnp.float32)
        final_normed = normalize(hidden, final_gain).astype(jnp.bfloat16)
        velocity = jnp.dot(final_normed, output_weight, preferred_element_type=jnp.float32)
        action_state = action_state - velocity / STEPS
    return action_state


def shards(
    prefix_hidden,
    prefix_lengths,
    action_noise,
    prefix_gain,
    key_weight,
    value_weight,
    input_weight,
    expert_gain,
    expert_query,
    expert_key,
    expert_value,
    expert_output,
    final_gain,
    output_weight,
):
    gathered = (
        lax.all_gather(expert_query, "wide", axis=0, tiled=True),
        lax.all_gather(expert_key, "wide", axis=0, tiled=True),
        lax.all_gather(expert_value, "wide", axis=0, tiled=True),
        lax.all_gather(expert_output, "wide", axis=0, tiled=True),
    )
    hidden = prefix_hidden[0]
    row_count = hidden.shape[0]
    normed = normalize(hidden.astype(jnp.float32), prefix_gain).astype(jnp.bfloat16)
    stacked = jnp.stack([key_weight, value_weight], 0)
    projected = jnp.einsum(
        "pd,kdc->pkc",
        normed,
        lax.all_gather(stacked, "wide", axis=1, tiled=True),
        preferred_element_type=jnp.float32,
    )
    positions = jnp.arange(row_count, dtype=jnp.float32)
    key_cache = (
        rotate(projected[:, 0].reshape(row_count, -1, HEAD), positions)
        .reshape(row_count, -1)
        .astype(jnp.bfloat16)
    )
    value_cache = projected[:, 1].astype(jnp.bfloat16)
    query_w, key_w, value_w, output_w = gathered
    action_state = expert_steps(
        action_noise[0],
        prefix_lengths[0],
        input_weight,
        expert_gain,
        query_w,
        key_w,
        value_w,
        output_w,
        final_gain,
        output_weight,
        key_cache,
        value_cache,
    )
    return action_state[None]


def solution(mesh):
    placed = (
        P(("groups", "wide"), None, None),
        P(("groups", "wide")),
        P(("groups", "wide"), None, None),
        P(),
        P("wide", None),
        P("wide", None),
        P(),
        P(),
        P("wide", None),
        P("wide", None),
        P("wide", None),
        P("wide", None),
        P(),
        P(),
    )
    return jax.shard_map(
        shards,
        mesh=mesh,
        in_specs=placed,
        out_specs=P(("groups", "wide"), None, None),
        check_vma=False,
    )
```

profile of v0, /device:TPU:0, one launch (start us, length us, event | category | flops | bytes accessed | tf_op | source)
XLA Modules:
  0.0 368.0 jit_solution(7898720133912089493)
XLA Ops:
  8.8 2.3 pad_maximum_fusion
  12.0 3.1 fusion
  19.0 31.2 %all-gather.10.cloned.1.call-done = bf16[1024,512]{1,0:T(8,128)(2,1)} async-done(((bf16[64,512]{1,0:T(8,128)(2,1)}), bf16[1024,512]{1,0:T(8,128)(2,1)}) %all-gather.10.cloned.1.call-update) | async-done | bytes 1048592 | tf_op jit(solution)/shard_map/all_gather | solution.py:135
  50.2 1.5 fusion.107
  51.9 37.4 %all-gather.12.cloned.1.call-done = bf16[1024,512]{1,0:T(8,128)(2,1)} async-done(((bf16[64,512]{1,0:T(8,128)(2,1)}), bf16[1024,512]{1,0:T(8,128)(2,1)}) %all-gather.12.cloned.1.call-update) | async-done | bytes 1048592 | tf_op jit(solution)/shard_map/all_gather | solution.py:136
  89.2 1.5 convolution_convert_fusion.3
  91.4 40.4 %all-gather.8.cloned.1.call-done = bf16[1024,1024]{1,0:T(8,128)(2,1)} async-done(((bf16[64,1024]{1,0:T(8,128)(2,1)}), bf16[1024,1024]{1,0:T(8,128)(2,1)}) %all-gather.8.cloned.1.call-update) | async-done | bytes 2097168 | tf_op jit(solution)/shard_map/all_gather | solution.py:134
  131.9 2.1 fusion.106
  134.6 124.5 %all-gather.6.cloned.1.call-done = bf16[2,8192,512]{2,1,0:T(8,128)(2,1)} async-done(((bf16[2,512,512]{2,1,0:T(8,128)(2,1)}), bf16[2,8192,512]{2,1,0:T(8,128)(2,1)}) %all-gather.6.cloned.1.call-update) | async-done | bytes 16777232 | tf_op jit(solution)/shard_map/all_gather | solution.py:146
  259.1 9.5 %fusion.4 = f32[256,2,512]{2,0,1:T(8,128)S(1)} fusion(bf16[2,8192,512]{2,1,0:T(8,128)(2,1)} %all-gather.6.cloned.1.call-done, bf16[1,256,8192]{2,1,0:T(8,128)(2,1)} %param.14, f32[8192]{0:T(1024)S(1)} %copy-done.58, f32[256]{0:T(256)S(1)} %add_rsqrt_fusion), kind=kOutput, calls=%fused_computation.6 | convolution fusion | flops 4303355904 | bytes 22053888 | tf_op jit(solution)/shard_map/pd,kdc->pkc/dot_general | solution.py:143
  271.2 29.5 %all-gather.14.cloned.1.call-done = bf16[1024,1024]{1,0:T(8,128)(2,1)} async-done(((bf16[64,1024]{1,0:T(8,128)(2,1)}), bf16[1024,1024]{1,0:T(8,128)(2,1)}) %all-gather.14.cloned.1.call-update) | async-done | bytes 2097168 | tf_op jit(solution)/shard_map/all_gather | solution.py:137
  300.8 2.2 multiply_reduce_fusion.6
  306.0 1.7 fusion.100
  308.6 1.6 reshape.311
  315.5 2.1 fusion.31
  318.5 1.5 reshape.312
  322.0 1.6 convert_element_type.174
  323.6 2.2 multiply_reduce_fusion.4
  331.1 1.6 reshape.314
  337.2 2.1 fusion.32
  340.2 1.5 reshape.315
  343.7 1.6 convert_element_type.184
  345.3 2.2 multiply_reduce_fusion.2
  354.5 2.3 fusion.33
  (245 shorter events, 45.8 us)
Async XLA Ops:
  6.5 9.1 %copy-start = (f32[32,1024]{1,0:T(8,128)S(1)}, f32[32,1024]{1,0:T(8,128)}, u32[]{:S(2)}) copy-start(f32[32,1024]{1,0:T(8,128)} %param.20) | copy-start | bytes 393220
  6.5 43.7 %all-gather.10.cloned.1.call-start = ((), (), s32[]{:S(2)}) async-start(), calls=%async_computation.2 | async-start | bytes 1114112 | tf_op jit(solution)/shard_map/all_gather | solution.py:135
  7.3 82.0 %all-gather.12.cloned.1.call-start = ((), (), s32[]{:S(2)}) async-start(), calls=%async_computation.3 | async-start | bytes 1114112 | tf_op jit(solution)/shard_map/all_gather | solution.py:136
  8.0 123.8 %all-gather.8.cloned.1.call-start = ((), (), s32[]{:S(2)}) async-start(), calls=%async_computation.1 | async-start | bytes 2228224 | tf_op jit(solution)/shard_map/all_gather | solution.py:134
  8.7 250.4 %all-gather.6.cloned.1.call-start = ((), (), s32[]{:S(2)}) async-start(), calls=%async_computation | async-start | bytes 17825792 | tf_op jit(solution)/shard_map/all_gather | solution.py:146
  11.1 289.7 %all-gather.14.cloned.1.call-start = ((), (), s32[]{:S(2)}) async-start(), calls=%async_computation.4 | async-start | bytes 2228224 | tf_op jit(solution)/shard_map/all_gather | solution.py:137
  12.0 6.9 %copy-start.41 = (f32[1024]{0:T(1024)S(1)}, f32[1024]{0:T(1024)}, u32[]{:S(2)}) copy-start(f32[1024]{0:T(1024)} %param.21) | copy-start | bytes 12292
  16.1 117.8 %copy-start.17 = (f32[50,1024]{1,0:T(8,128)}, f32[50,1024]{1,0:T(8,128)S(1)}, u32[]{:S(2)}) copy-start(f32[50,1024]{1,0:T(8,128)S(1)} %get-tuple-element.38) | copy-start | bytes 614404
  17.0 117.0 %copy-start.7 = (f32[50,64]{1,0:T(8,128)}, f32[50,64]{1,0:T(8,128)S(1)}, u32[]{:S(2)}) copy-start(f32[50,64]{1,0:T(8,128)S(1)} %get-tuple-element.33) | copy-start | bytes 38404
  17.0 117.0 %copy-start.12 = (f32[50,64]{1,0:T(8,128)}, f32[50,64]{1,0:T(8,128)S(1)}, u32[]{:S(2)}) copy-start(f32[50,64]{1,0:T(8,128)S(1)} %get-tuple-element.34) | copy-start | bytes 38404
  17.0 252.6 %copy-start.53 = (pred[256]{0:T(512)(128)(4,1)}, pred[256]{0:T(512)(128)(4,1)S(1)}, u32[]{:S(2)}) copy-start(pred[256]{0:T(512)(128)(4,1)S(1)} %iota_compare_fusion) | copy-start | bytes 772
  91.4 167.7 %copy-start.58 = (f32[8192]{0:T(1024)S(1)}, f32[8192]{0:T(1024)}, u32[]{:S(2)}) copy-start(f32[8192]{0:T(1024)} %param.17) | copy-start | bytes 98308
  270.1 30.6 %copy-start.18 = (f32[50,1024]{1,0:T(8,128)S(1)}, f32[50,1024]{1,0:T(8,128)}, u32[]{:S(2)}) copy-start(f32[50,1024]{1,0:T(8,128)} %copy-done.17) | copy-start | bytes 614404
  270.8 32.2 %copy-start.30 = (bf16[1024,32]{0,1:T(8,128)(2,1)S(1)}, bf16[1024,32]{0,1:T(8,128)(2,1)}, u32[]{:S(2)}) copy-start(bf16[1024,32]{0,1:T(8,128)(2,1)} %param.27) | copy-start | bytes 196612
  270.8 32.2 %copy-start.45 = (f32[1,50,32]{1,2,0:T(8,128)S(1)}, f32[1,50,32]{1,2,0:T(8,128)}, u32[]{:S(2)}) copy-start(f32[1,50,32]{1,2,0:T(8,128)} %param.16) | copy-start | bytes 19204
  270.8 32.2 %copy-start.46 = (f32[1024]{0:T(1024)S(1)}, f32[1024]{0:T(1024)}, u32[]{:S(2)}) copy-start(f32[1024]{0:T(1024)} %param.26) | copy-start | bytes 12292
  270.8 32.4 %copy-start.52 = (f32[1024]{0:T(1024)S(1)}, f32[1024]{0:T(1024)}, u32[]{:S(2)}) copy-start(f32[1024]{0:T(1024)} %pad_maximum_fusion.2) | copy-start | bytes 12292
  271.1 32.7 %copy-start.42 = (f32[1024]{0:T(1024)S(1)}, f32[1024]{0:T(1024)}, u32[]{:S(2)}) copy-start(f32[1024]{0:T(1024)} %param.21) | copy-start | bytes 12292
  271.1 33.4 %copy-start.1 = (bf16[1024,1024]{1,0:T(8,128)(2,1)S(1)}, bf16[1024,1024]{1,0:T(8,128)(2,1)}, u32[]{:S(2)}) copy-start(bf16[1024,1024]{1,0:T(8,128)(2,1)} %all-gather.8.cloned.1.call-done) | copy-start | bytes 6291460
  310.2 7.4 %copy-start.3 = (bf16[1024,512]{1,0:T(8,128)(2,1)S(1)}, bf16[1024,512]{1,0:T(8,128)(2,1)}, u32[]{:S(2)}) copy-start(bf16[1024,512]{1,0:T(8,128)(2,1)} %all-gather.12.cloned.1.call-done) | copy-start | bytes 3145732
  310.2 7.4 %copy-start.26 = (bf16[50,1024]{1,0:T(8,128)(2,1)S(1)}, bf16[50,1024]{1,0:T(8,128)(2,1)}, u32[]{:S(2)}) copy-start(bf16[50,1024]{1,0:T(8,128)(2,1)} %copy-done.25) | copy-start | bytes 307204
  332.6 6.7 %copy-start.28 = (bf16[50,1024]{1,0:T(8,128)(2,1)S(1)}, bf16[50,1024]{1,0:T(8,128)(2,1)}, u32[]{:S(2)}) copy-start(bf16[50,1024]{1,0:T(8,128)(2,1)} %copy-done.27) | copy-start | bytes 307204
  354.5 5.5 %copy-start.2 = (bf16[1024,1024]{1,0:T(8,128)(2,1)S(1)}, bf16[1024,1024]{1,0:T(8,128)(2,1)}, u32[]{:S(2)}) copy-start(bf16[1024,1024]{1,0:T(8,128)(2,1)} %all-gather.14.cloned.1.call-done) | copy-start | bytes 6291460
  354.5 5.5 %copy-start.20 = (f32[50,1024]{1,0:T(8,128)S(1)}, f32[50,1024]{1,0:T(8,128)}, u32[]{:S(2)}) copy-start(f32[50,1024]{1,0:T(8,128)} %copy-done.19) | copy-start | bytes 614404
  (40 other events, 77.0 us)
Sparse Core Ops, SparseCore 0:
  9.5 40.6 all-gather.9
  52.4 36.8 all-gather.11
  91.4 40.4 all-gather.7
  133.9 125.1 all-gather.5
  261.1 39.6 all-gather.13
where the time goes:
time: 369 us; the launch traced here: 368 us
  waiting for transfers between devices  266 us (72%)
  matrix products  50.5 us (14%)
  local copies, waits for them, and re-layouts  20.1 us (5%)
  other arithmetic  16.4 us (4%)
  between operations  15.1 us (4%)
    all_gather x1, waiting for transfers between devices, shards(): lax.all_gather(stacked, 'wide', axis=1, tiled=True)  124 us
    all_gather x1, waiting for transfers between devices, shards(): lax.all_gather(expert_query, 'wide', axis=0, tiled=True)  40.4 us
    all_gather x1, waiting for transfers between devices, shards(): lax.all_gather(expert_value, 'wide', axis=0, tiled=True)  37.4 us
    all_gather x1, waiting for transfers between devices, shards(): lax.all_gather(expert_key, 'wide', axis=0, tiled=True)  31.2 us
    all_gather x1, waiting for transfers between devices, shards(): lax.all_gather(expert_output, 'wide', axis=0, tiled=True)  29.5 us
    dot_general x1, matrix products, shards(): jnp.einsum('pd,kdc->pkc', normed, lax.all_gather(stacked, 'wide', axis=1,...  9.54 us
  transfers between devices with their start and end apart: 5, of which 5 were waited for; matrix products, arithmetic and copies ran while one was open for 7% of the time, Pallas kernels for 0%

commit v1 on v0

--- a/solution.py
+++ b/solution.py
@@ -7,6 +7,22 @@
 STEPS = 4
 rope_base = 1000000.0
 norm_eps = 1e-06
+
+
+def gather_around(x, axis, dim):
+    ways, here, step = (lax.axis_size(axis), lax.axis_index(axis), x.shape[dim])
+    shape = [n * ways if d == dim else n for d, n in enumerate(x.shape)]
+    full = lax.dynamic_update_slice_in_dim(jnp.zeros(shape, x.dtype), x, here * step, axis=dim)
+    going_up = going_down = x
+    for far in range(1, ways // 2 + 1):
+        going_up = lax.ppermute(going_up, axis, [(d, (d + 1) % ways) for d in range(ways)])
+        full = lax.dynamic_update_slice_in_dim(full, going_up, (here - far) % ways * step, axis=dim)
+        if 2 * far < ways:
+            going_down = lax.ppermute(going_down, axis, [(d, (d - 1) % ways) for d in range(ways)])
+            full = lax.dynamic_update_slice_in_dim(
+                full, going_down, (here + far) % ways * step, axis=dim
+            )
+    return full
 
 
 def normalize(values, norm_gain):
@@ -134,7 +150,7 @@
         lax.all_gather(expert_query, "wide", axis=0, tiled=True),
         lax.all_gather(expert_key, "wide", axis=0, tiled=True),
         lax.all_gather(expert_value, "wide", axis=0, tiled=True),
-        lax.all_gather(expert_output, "wide", axis=0, tiled=True),
+        gather_around(expert_output, "wide", 0),
     )
     hidden = prefix_hidden[0]
     row_count = hidden.shape[0]

time: 369 us -> 344 us (0.932)
  waiting for transfers between devices: 266 us -> 204 us
  starting transfers between devices: 0.16 us -> 32.4 us
  other arithmetic: 16.4 us -> 20.1 us
    ppermute x0 -> x15, starting transfers between devices: none -> 32.3 us  [the longest x7 31.7 us: gather_around(): lax.ppermute(going_down, axis, [(d, (d - 1) % ways) for d in range(ways)])]
    all_gather x1, waiting for transfers between devices: 31.2 us -> 0.02 us  [shards(): lax.all_gather(expert_key, 'wide', axis=0, tiled=True)]
    all_gather x1 -> x0, waiting for transfers between devices: 29.5 us -> none  [shards(): lax.all_gather(expert_output, 'wide', axis=0, tiled=True)]
    ppermute x0 -> x15, waiting for transfers between devices: none -> 23.9 us  [the longest x8 23.9 us: gather_around(): lax.ppermute(going_up, axis, [(d, (d + 1) % ways) for d in range(ways)])]
    all_gather x1, waiting for transfers between devices: 37.4 us -> 13.8 us  [shards(): lax.all_gather(expert_value, 'wide', axis=0, tiled=True)]
  transfers between devices with their start and end apart: 5 -> 19, of which waited for: 5 -> 10; matrix products, arithmetic and copies ran while one was open for 7% -> 5% of each run, Pallas kernels for 0% -> 0%
where the time goes in v1:
time: 344 us; the launch traced here: 343 us
  waiting for transfers between devices  204 us (59%)
  matrix products  51.9 us (15%)
  starting transfers between devices  32.4 us (9%)
  other arithmetic  20.1 us (6%)
  local copies, waits for them, and re-layouts  18.7 us (5%)
  between operations  15.5 us (5%)
    all_gather x1, waiting for transfers between devices, shards(): lax.all_gather(stacked, 'wide', axis=1, tiled=True)  124 us
    all_gather x1, waiting for transfers between devices, shards(): lax.all_gather(expert_query, 'wide', axis=0, tiled=True)  40.3 us
    ppermute x7, starting transfers between devices, gather_around(): lax.ppermute(going_down, axis, [(d, (d - 1) % ways) for d in range(ways)])  31.7 us
    ppermute x8, waiting for transfers between devices, gather_around(): lax.ppermute(going_up, axis, [(d, (d + 1) % ways) for d in range(ways)])  23.9 us
    all_gather x1, waiting for transfers between devices, shards(): lax.all_gather(expert_value, 'wide', axis=0, tiled=True)  13.8 us
    dot_general x1, matrix products, shards(): jnp.einsum('pd,kdc->pkc', normed, lax.all_gather(stacked, 'wide', axis=1,...  9.61 us
    dot_general x4, matrix products, attend(): jnp.einsum('grcp,pgh->cgrh', prefix_prob, prefix_values, preferred_elemen...  7.67 us
  transfers between devices with their start and end apart: 19, of which 10 were waited for; matrix products, arithmetic and copies ran while one was open for 5% of the time, Pallas kernels for 0%

profile of v1, /device:TPU:0, one launch (start us, length us, event | category | flops | bytes accessed | tf_op | source)
XLA Modules:
  0.0 342.7 jit_solution(7726771379037573603)
XLA Ops:
  8.8 2.3 pad_maximum_fusion
  11.7 5.0 %collective-permute-start.1 = (bf16[64,1024]{1,0:T(8,128)(2,1)S(1)}, bf16[64,1024]{1,0:T(8,128)(2,1)S(1)}, u32[]{:S(2)}, u32[]{:S(2)}) collective-permute-start(bf16[64,1024]{1,0:T(8,128)(2,1)S(1)} %copy-done.42), channel_id=1, source_target_pairs={{0,15},{1,0},{2,1},{3,2},{4,3},{5,4},{6,5},{7,6},{8,7},{9,8},{10,9... | collective-permute-start | bytes 393224 | tf_op jit(solution)/shard_map/ppermute | solution.py:21
  20.0 3.2 fusion
  25.4 4.4 %collective-permute-start.3 = (bf16[64,1024]{1,0:T(8,128)(2,1)S(1)}, bf16[64,1024]{1,0:T(8,128)(2,1)S(1)}, u32[]{:S(2)}, u32[]{:S(2)}) collective-permute-start(bf16[64,1024]{1,0:T(8,128)(2,1)S(1)} %collective-permute-done.1), channel_id=1, source_target_pairs={{0,15},{1,0},{2,1},{3,2},{4,3},{5,4},{6,5},{7,6},{8,7},{9,8},{10,9... | collective-permute-start | bytes 393224 | tf_op jit(solution)/shard_map/ppermute | solution.py:21
  29.9 2.8 collective-permute-done.2
  32.7 4.4 %collective-permute-start.5 = (bf16[64,1024]{1,0:T(8,128)(2,1)S(1)}, bf16[64,1024]{1,0:T(8,128)(2,1)S(1)}, u32[]{:S(2)}, u32[]{:S(2)}) collective-permute-start(bf16[64,1024]{1,0:T(8,128)(2,1)S(1)} %collective-permute-done.3), channel_id=1, source_target_pairs={{0,15},{1,0},{2,1},{3,2},{4,3},{5,4},{6,5},{7,6},{8,7},{9,8},{10,9... | collective-permute-start | bytes 393224 | tf_op jit(solution)/shard_map/ppermute | solution.py:21
  37.2 2.7 collective-permute-done.4
  39.9 4.5 %collective-permute-start.7 = (bf16[64,1024]{1,0:T(8,128)(2,1)S(1)}, bf16[64,1024]{1,0:T(8,128)(2,1)S(1)}, u32[]{:S(2)}, u32[]{:S(2)}) collective-permute-start(bf16[64,1024]{1,0:T(8,128)(2,1)S(1)} %collective-permute-done.5), channel_id=1, source_target_pairs={{0,15},{1,0},{2,1},{3,2},{4,3},{5,4},{6,5},{7,6},{8,7},{9,8},{10,9... | collective-permute-start | bytes 393224 | tf_op jit(solution)/shard_map/ppermute | solution.py:21
  44.4 2.9 collective-permute-done.6
  47.3 4.4 %collective-permute-start.9 = (bf16[64,1024]{1,0:T(8,128)(2,1)S(1)}, bf16[64,1024]{1,0:T(8,128)(2,1)S(1)}, u32[]{:S(2)}, u32[]{:S(2)}) collective-permute-start(bf16[64,1024]{1,0:T(8,128)(2,1)S(1)} %collective-permute-done.7), channel_id=1, source_target_pairs={{0,15},{1,0},{2,1},{3,2},{4,3},{5,4},{6,5},{7,6},{8,7},{9,8},{10,9... | collective-permute-start | bytes 393224 | tf_op jit(solution)/shard_map/ppermute | solution.py:21
  51.8 2.7 collective-permute-done.8
  54.5 4.4 %collective-permute-start.11 = (bf16[64,1024]{1,0:T(8,128)(2,1)S(1)}, bf16[64,1024]{1,0:T(8,128)(2,1)S(1)}, u32[]{:S(2)}, u32[]{:S(2)}) collective-permute-start(bf16[64,1024]{1,0:T(8,128)(2,1)S(1)} %collective-permute-done.9), channel_id=1, source_target_pairs={{0,15},{1,0},{2,1},{3,2},{4,3},{5,4},{6,5},{7,6},{8,7},{9,8},{10,9... | collective-permute-start | bytes 393224 | tf_op jit(solution)/shard_map/ppermute | solution.py:21
  59.0 2.7 collective-permute-done.10
  61.7 4.4 %collective-permute-start.13 = (bf16[64,1024]{1,0:T(8,128)(2,1)S(1)}, bf16[64,1024]{1,0:T(8,128)(2,1)S(1)}, u32[]{:S(2)}, u32[]{:S(2)}) collective-permute-start(bf16[64,1024]{1,0:T(8,128)(2,1)S(1)} %collective-permute-done.11), channel_id=1, source_target_pairs={{0,15},{1,0},{2,1},{3,2},{4,3},{5,4},{6,5},{7,6},{8,7},{9,8},{10,9... | collective-permute-start | bytes 393224 | tf_op jit(solution)/shard_map/ppermute | solution.py:21
  66.2 3.1 collective-permute-done.12
  69.3 7.0 %collective-permute-done.14 = bf16[64,1024]{1,0:T(8,128)(2,1)S(1)} collective-permute-done((bf16[64,1024]{1,0:T(8,128)(2,1)S(1)}, bf16[64,1024]{1,0:T(8,128)(2,1)S(1)}, u32[]{:S(2)}, u32[]{:S(2)}) %collective-permute-start.14) | collective-permute-done | bytes 131104 | tf_op jit(solution)/shard_map/ppermute | solution.py:18
  77.9 13.8 %all-gather.11.cloned.1.call-done = bf16[1024,512]{1,0:T(8,128)(2,1)} async-done(((bf16[64,512]{1,0:T(8,128)(2,1)}), bf16[1024,512]{1,0:T(8,128)(2,1)}) %all-gather.11.cloned.1.call-update) | async-done | bytes 1048592 | tf_op jit(solution)/shard_map/all_gather | solution.py:152
  94.0 40.3 %all-gather.7.cloned.1.call-done = bf16[1024,1024]{1,0:T(8,128)(2,1)} async-done(((bf16[64,1024]{1,0:T(8,128)(2,1)}), bf16[1024,1024]{1,0:T(8,128)(2,1)}) %all-gather.7.cloned.1.call-update) | async-done | bytes 2097168 | tf_op jit(solution)/shard_map/all_gather | solution.py:150
  134.3 2.1 fusion.106
  137.8 123.8 %all-gather.5.cloned.1.call-done = bf16[2,8192,512]{2,1,0:T(8,128)(2,1)} async-done(((bf16[2,512,512]{2,1,0:T(8,128)(2,1)}), bf16[2,8192,512]{2,1,0:T(8,128)(2,1)}) %all-gather.5.cloned.1.call-update) | async-done | bytes 16777232 | tf_op jit(solution)/shard_map/all_gather | solution.py:162
  261.6 9.6 %fusion.4 = f32[256,2,512]{2,0,1:T(8,128)S(1)} fusion(bf16[2,8192,512]{2,1,0:T(8,128)(2,1)} %all-gather.5.cloned.1.call-done, bf16[1,256,8192]{2,1,0:T(8,128)(2,1)} %param.14, f32[8192]{0:T(1024)S(1)} %copy-done.61, f32[256]{0:T(256)S(1)} %add_rsqrt_fusion), kind=kOutput, calls=%fused_computation.6 | convolution fusion | flops 4303355904 | bytes 22053888 | tf_op jit(solution)/shard_map/pd,kdc->pkc/dot_general | solution.py:159
  289.1 2.1 fusion.31
  309.7 2.1 fusion.32
  329.2 2.1 fusion.33
  (295 shorter events, 70.1 us)
Async XLA Ops:
  6.5 69.8 %all-gather.9.cloned.1.call-start = ((), (), s32[]{:S(2)}) async-start(), calls=%async_computation.2 | async-start | bytes 1114112 | tf_op jit(solution)/shard_map/all_gather | solution.py:151
  7.3 84.4 %all-gather.11.cloned.1.call-start = ((), (), s32[]{:S(2)}) async-start(), calls=%async_computation.3 | async-start | bytes 1114112 | tf_op jit(solution)/shard_map/all_gather | solution.py:152
  8.0 126.3 %all-gather.7.cloned.1.call-start = ((), (), s32[]{:S(2)}) async-start(), calls=%async_computation.1 | async-start | bytes 2228224 | tf_op jit(solution)/shard_map/all_gather | solution.py:150
  8.7 252.8 %all-gather.5.cloned.1.call-start = ((), (), s32[]{:S(2)}) async-start(), calls=%async_computation | async-start | bytes 17825792 | tf_op jit(solution)/shard_map/all_gather | solution.py:162
  11.1 14.2 %collective-permute-start = (bf16[64,1024]{1,0:T(8,128)(2,1)S(1)}, bf16[64,1024]{1,0:T(8,128)(2,1)S(1)}, u32[]{:S(2)}, u32[]{:S(2)}) collective-permute-start(bf16[64,1024]{1,0:T(8,128)(2,1)S(1)} %copy-done.42), channel_id=1, source_target_pairs={{0,1},{1,2},{2,3},{3,4},{4,5},{5,6},{6,7},{7,8},{8,9},{9,10},{10,1... | collective-permute-start | bytes 393224 | tf_op jit(solution)/shard_map/ppermute | solution.py:18
  11.7 13.7 %collective-permute-start.1 = (bf16[64,1024]{1,0:T(8,128)(2,1)S(1)}, bf16[64,1024]{1,0:T(8,128)(2,1)S(1)}, u32[]{:S(2)}, u32[]{:S(2)}) collective-permute-start(bf16[64,1024]{1,0:T(8,128)(2,1)S(1)} %copy-done.42), channel_id=1, source_target_pairs={{0,15},{1,0},{2,1},{3,2},{4,3},{5,4},{6,5},{7,6},{8,7},{9,8},{10,9... | collective-permute-start | bytes 393224 | tf_op jit(solution)/shard_map/ppermute | solution.py:21
  23.4 256.8 %copy-start.8 = (f32[50,64]{1,0:T(8,128)}, f32[50,64]{1,0:T(8,128)S(1)}, u32[]{:S(2)}) copy-start(f32[50,64]{1,0:T(8,128)S(1)} %get-tuple-element.33) | copy-start | bytes 38404
  23.4 256.8 %copy-start.11 = (f32[50,64]{1,0:T(8,128)}, f32[50,64]{1,0:T(8,128)S(1)}, u32[]{:S(2)}) copy-start(f32[50,64]{1,0:T(8,128)S(1)} %get-tuple-element.34) | copy-start | bytes 38404
  24.8 249.1 %copy-start.55 = (pred[256]{0:T(512)(128)(4,1)}, pred[256]{0:T(512)(128)(4,1)S(1)}, u32[]{:S(2)}) copy-start(pred[256]{0:T(512)(128)(4,1)S(1)} %iota_compare_fusion) | copy-start | bytes 772
  25.4 7.4 %collective-permute-start.2 = (bf16[64,1024]{1,0:T(8,128)(2,1)S(1)}, bf16[64,1024]{1,0:T(8,128)(2,1)S(1)}, u32[]{:S(2)}, u32[]{:S(2)}) collective-permute-start(bf16[64,1024]{1,0:T(8,128)(2,1)S(1)} %collective-permute-done), channel_id=1, source_target_pairs={{0,1},{1,2},{2,3},{3,4},{4,5},{5,6},{6,7},{7,8},{8,9},{9,10},{10,1... | collective-permute-start | bytes 393224 | tf_op jit(solution)/shard_map/ppermute | solution.py:18
  25.4 7.3 %collective-permute-start.3 = (bf16[64,1024]{1,0:T(8,128)(2,1)S(1)}, bf16[64,1024]{1,0:T(8,128)(2,1)S(1)}, u32[]{:S(2)}, u32[]{:S(2)}) collective-permute-start(bf16[64,1024]{1,0:T(8,128)(2,1)S(1)} %collective-permute-done.1), channel_id=1, source_target_pairs={{0,15},{1,0},{2,1},{3,2},{4,3},{5,4},{6,5},{7,6},{8,7},{9,8},{10,9... | collective-permute-start | bytes 393224 | tf_op jit(solution)/shard_map/ppermute | solution.py:21
  32.7 7.2 %collective-permute-start.4 = (bf16[64,1024]{1,0:T(8,128)(2,1)S(1)}, bf16[64,1024]{1,0:T(8,128)(2,1)S(1)}, u32[]{:S(2)}, u32[]{:S(2)}) collective-permute-start(bf16[64,1024]{1,0:T(8,128)(2,1)S(1)} %collective-permute-done.2), channel_id=1, source_target_pairs={{0,1},{1,2},{2,3},{3,4},{4,5},{5,6},{6,7},{7,8},{8,9},{9,10},{10,1... | collective-permute-start | bytes 393224 | tf_op jit(solution)/shard_map/ppermute | solution.py:18
  32.7 7.2 %collective-permute-start.5 = (bf16[64,1024]{1,0:T(8,128)(2,1)S(1)}, bf16[64,1024]{1,0:T(8,128)(2,1)S(1)}, u32[]{:S(2)}, u32[]{:S(2)}) collective-permute-start(bf16[64,1024]{1,0:T(8,128)(2,1)S(1)} %collective-permute-done.3), channel_id=1, source_target_pairs={{0,15},{1,0},{2,1},{3,2},{4,3},{5,4},{6,5},{7,6},{8,7},{9,8},{10,9... | collective-permute-start | bytes 393224 | tf_op jit(solution)/shard_map/ppermute | solution.py:21
  39.9 7.4 %collective-permute-start.6 = (bf16[64,1024]{1,0:T(8,128)(2,1)S(1)}, bf16[64,1024]{1,0:T(8,128)(2,1)S(1)}, u32[]{:S(2)}, u32[]{:S(2)}) collective-permute-start(bf16[64,1024]{1,0:T(8,128)(2,1)S(1)} %collective-permute-done.4), channel_id=1, source_target_pairs={{0,1},{1,2},{2,3},{3,4},{4,5},{5,6},{6,7},{7,8},{8,9},{9,10},{10,1... | collective-permute-start | bytes 393224 | tf_op jit(solution)/shard_map/ppermute | solution.py:18
  39.9 7.4 %collective-permute-start.7 = (bf16[64,1024]{1,0:T(8,128)(2,1)S(1)}, bf16[64,1024]{1,0:T(8,128)(2,1)S(1)}, u32[]{:S(2)}, u32[]{:S(2)}) collective-permute-start(bf16[64,1024]{1,0:T(8,128)(2,1)S(1)} %collective-permute-done.5), channel_id=1, source_target_pairs={{0,15},{1,0},{2,1},{3,2},{4,3},{5,4},{6,5},{7,6},{8,7},{9,8},{10,9... | collective-permute-start | bytes 393224 | tf_op jit(solution)/shard_map/ppermute | solution.py:21
  47.3 7.2 %collective-permute-start.8 = (bf16[64,1024]{1,0:T(8,128)(2,1)S(1)}, bf16[64,1024]{1,0:T(8,128)(2,1)S(1)}, u32[]{:S(2)}, u32[]{:S(2)}) collective-permute-start(bf16[64,1024]{1,0:T(8,128)(2,1)S(1)} %collective-permute-done.6), channel_id=1, source_target_pairs={{0,1},{1,2},{2,3},{3,4},{4,5},{5,6},{6,7},{7,8},{8,9},{9,10},{10,1... | collective-permute-start | bytes 393224 | tf_op jit(solution)/shard_map/ppermute | solution.py:18
  47.3 7.2 %collective-permute-start.9 = (bf16[64,1024]{1,0:T(8,128)(2,1)S(1)}, bf16[64,1024]{1,0:T(8,128)(2,1)S(1)}, u32[]{:S(2)}, u32[]{:S(2)}) collective-permute-start(bf16[64,1024]{1,0:T(8,128)(2,1)S(1)} %collective-permute-done.7), channel_id=1, source_target_pairs={{0,15},{1,0},{2,1},{3,2},{4,3},{5,4},{6,5},{7,6},{8,7},{9,8},{10,9... | collective-permute-start | bytes 393224 | tf_op jit(solution)/shard_map/ppermute | solution.py:21
  54.5 7.2 %collective-permute-start.10 = (bf16[64,1024]{1,0:T(8,128)(2,1)S(1)}, bf16[64,1024]{1,0:T(8,128)(2,1)S(1)}, u32[]{:S(2)}, u32[]{:S(2)}) collective-permute-start(bf16[64,1024]{1,0:T(8,128)(2,1)S(1)} %collective-permute-done.8), channel_id=1, source_target_pairs={{0,1},{1,2},{2,3},{3,4},{4,5},{5,6},{6,7},{7,8},{8,9},{9,10},{10,1... | collective-permute-start | bytes 393224 | tf_op jit(solution)/shard_map/ppermute | solution.py:18
  54.5 7.2 %collective-permute-start.11 = (bf16[64,1024]{1,0:T(8,128)(2,1)S(1)}, bf16[64,1024]{1,0:T(8,128)(2,1)S(1)}, u32[]{:S(2)}, u32[]{:S(2)}) collective-permute-start(bf16[64,1024]{1,0:T(8,128)(2,1)S(1)} %collective-permute-done.9), channel_id=1, source_target_pairs={{0,15},{1,0},{2,1},{3,2},{4,3},{5,4},{6,5},{7,6},{8,7},{9,8},{10,9... | collective-permute-start | bytes 393224 | tf_op jit(solution)/shard_map/ppermute | solution.py:21
  61.7 7.6 %collective-permute-start.12 = (bf16[64,1024]{1,0:T(8,128)(2,1)S(1)}, bf16[64,1024]{1,0:T(8,128)(2,1)S(1)}, u32[]{:S(2)}, u32[]{:S(2)}) collective-permute-start(bf16[64,1024]{1,0:T(8,128)(2,1)S(1)} %collective-permute-done.10), channel_id=1, source_target_pairs={{0,1},{1,2},{2,3},{3,4},{4,5},{5,6},{6,7},{7,8},{8,9},{9,10},{10,1... | collective-permute-start | bytes 393224 | tf_op jit(solution)/shard_map/ppermute | solution.py:18
  61.7 7.6 %collective-permute-start.13 = (bf16[64,1024]{1,0:T(8,128)(2,1)S(1)}, bf16[64,1024]{1,0:T(8,128)(2,1)S(1)}, u32[]{:S(2)}, u32[]{:S(2)}) collective-permute-start(bf16[64,1024]{1,0:T(8,128)(2,1)S(1)} %collective-permute-done.11), channel_id=1, source_target_pairs={{0,15},{1,0},{2,1},{3,2},{4,3},{5,4},{6,5},{7,6},{8,7},{9,8},{10,9... | collective-permute-start | bytes 393224 | tf_op jit(solution)/shard_map/ppermute | solution.py:21
  69.2 7.1 %collective-permute-start.14 = (bf16[64,1024]{1,0:T(8,128)(2,1)S(1)}, bf16[64,1024]{1,0:T(8,128)(2,1)S(1)}, u32[]{:S(2)}, u32[]{:S(2)}) collective-permute-start(bf16[64,1024]{1,0:T(8,128)(2,1)S(1)} %collective-permute-done.12), channel_id=1, source_target_pairs={{0,1},{1,2},{2,3},{3,4},{4,5},{5,6},{6,7},{7,8},{8,9},{9,10},{10,1... | collective-permute-start | bytes 393224 | tf_op jit(solution)/shard_map/ppermute | solution.py:18
  94.0 167.6 %copy-start.61 = (f32[8192]{0:T(1024)S(1)}, f32[8192]{0:T(1024)}, u32[]{:S(2)}) copy-start(f32[8192]{0:T(1024)} %param.17) | copy-start | bytes 98308
  136.8 134.4 %copy-start.31 = (bf16[50,8,128]{2,0,1:T(8,128)(2,1)}, bf16[50,8,128]{2,0,1:T(8,128)(2,1)S(1)}, u32[]{:S(2)}) copy-start(bf16[50,8,128]{2,0,1:T(8,128)(2,1)S(1)} %copy.37) | copy-start | bytes 307204
  (57 other events, 166.9 us)
Sparse Core Ops, SparseCore 0:
  9.5 42.8 all-gather.8
  54.5 37.1 all-gather.10
  93.9 40.4 all-gather.6
  136.4 125.1 all-gather.4
